TPU v7x, 512 devices: a whole 4x8x8 slice. The times are simulated.
512 devices in a mesh: shell: 8 (over z), row: 4 (over x_hi, core), col: 16 (over x_lo, y).
Axes of the slice: x: 4 (x_hi: 2, x_lo: 2; x = x_hi * 2 + x_lo), y: 8, z: 8, core: 2. Of those that a mesh axis runs over, the one named last changes fastest.
Arguments:
- left_basis: bfloat16 [2, 4096, 6144], P(None, 'row', 'shell'), may hold values from -6 to 6
- right_basis: bfloat16 [2, 6144, 8192], P(None, 'shell', 'col'), may hold values from -0.078125 to 0.078125
- point_weight: float32 [6144], P('shell'), may hold values from 0.3 to 3
- shell_index: int32 [6144], P('shell'), may hold values from 0 to 11
- green_table: float32 [12, 2], replicated, may hold values from -4 to 4
- pivot_rows: int32 [512], replicated, may hold values from 0 to 4095, as said below
- diag_inverse: bfloat16 [2, 512, 512], replicated, may hold values from -0.005859375 to 0.005859375
Outputs:
- factored: float32 [2, 4, 8, 128, 8192], P(None, 'row', 'shell', None, 'col')
Inputs may be any that keep to these rules, and one draw needn't show every extreme that they name: `pivot_rows`: 512 distinct matrix rows.
All inputs are finite; a program needn't handle non-finite values.
Results may differ from a plain program's by a relative error of at most 0.0056.
Values may be sent and summed in bfloat16 or wider, within the bound.
No kernel may reach another device: no remote copies, remote signals or barrier semaphores. Data moves between devices by JAX's collectives and lax.ppermute only.
A program may use at most 128 MiB of HBM per device.

v0:
```python
import jax
import jax.numpy as jnp
from jax import lax
from jax.sharding import PartitionSpec as P


def broadcast(block, axis, source):
    block = jnp.where(lax.axis_index(axis) == source, block, jnp.zeros_like(block))
    return lax.psum(block, axis)


def complex_block(real_part, imag_part):
    upper_half = jnp.concatenate([real_part, imag_part], axis=1)
    lower_half = jnp.concatenate([-imag_part, real_part], axis=1)
    return jnp.concatenate([upper_half, lower_half], axis=0)


def weigh_points(right_basis, point_weight, shell_index, green_table):
    shells_count = green_table.shape[0]
    matches = shell_index[:, None] == jnp.arange(shells_count, dtype=jnp.int32)[None, :]
    green_real = jnp.sum(jnp.where(matches, green_table[None, :, 0], 0.0), axis=1)
    green_imag = jnp.sum(jnp.where(matches, green_table[None, :, 1], 0.0), axis=1)
    weight_real = point_weight * green_real
    weight_imag = point_weight * green_imag
    basis_real = right_basis[0].astype(jnp.float32)
    basis_imag = right_basis[1].astype(jnp.float32)
    weighted_real = (weight_real[:, None] * basis_real - weight_imag[:, None] * basis_imag).astype(
        jnp.bfloat16
    )
    weighted_imag = (weight_real[:, None] * basis_imag + weight_imag[:, None] * basis_real).astype(
        jnp.bfloat16
    )
    return (weighted_real, weighted_imag)


def reduce_tiles(term_rows, owned_rows):
    return lax.psum_scatter(
        term_rows(jnp.int32(0), owned_rows * lax.axis_size("shell")),
        "shell",
        scatter_dimension=0,
        tiled=True,
    )


def pick_rows(matrix_rows, pivot_rows, row_base):
    held_rows = matrix_rows.shape[0]
    local_index = pivot_rows - row_base
    inside = (local_index >= 0) & (local_index < held_rows)
    picked = jnp.take(matrix_rows, jnp.clip(local_index, 0, held_rows - 1), axis=0)
    return jnp.where(inside[:, None], picked, 0.0)


def select_pivots(coupling, pivot_rows, row_base):
    picked = pick_rows(coupling, pivot_rows, row_base).astype(jnp.bfloat16)
    return lax.psum(picked, ("shell", "row")).astype(jnp.float32).astype(jnp.bfloat16)


def body(left_basis, right_basis, point_weight, shell_index, green_table, pivot_rows, diag_inverse):
    shells = lax.axis_size("shell")
    owned_rows = left_basis.shape[1] // shells
    panel_width = right_basis.shape[2]
    weighted_real, weighted_imag = weigh_points(right_basis, point_weight, shell_index, green_table)
    grid_row = lax.axis_index("row")
    shell_rank = lax.axis_index("shell")
    row_base = (grid_row * shells + shell_rank) * owned_rows
    left_stack = jnp.concatenate([left_basis[0], left_basis[1]], axis=1)
    right_stack = complex_block(weighted_real, weighted_imag)

    def from_bases(first_row, row_count):
        return jnp.dot(left_stack, right_stack, preferred_element_type=jnp.float32)

    coupling = reduce_tiles(from_bases, owned_rows)
    pivot_sum = select_pivots(coupling, pivot_rows, row_base)
    panel_real = coupling[:, :panel_width]
    panel_imag = coupling[:, panel_width:]
    inverse_real = diag_inverse[0].astype(jnp.float32)
    inverse_imag = diag_inverse[1].astype(jnp.float32)
    highest = lax.Precision.HIGHEST
    mult_real = (
        jnp.dot(panel_real, inverse_real, precision=highest, preferred_element_type=jnp.float32)
        - jnp.dot(panel_imag, inverse_imag, precision=highest, preferred_element_type=jnp.float32)
    ).astype(jnp.bfloat16)
    mult_imag = (
        jnp.dot(panel_real, inverse_imag, precision=highest, preferred_element_type=jnp.float32)
        + jnp.dot(panel_imag, inverse_real, precision=highest, preferred_element_type=jnp.float32)
    ).astype(jnp.bfloat16)
    multipliers = jnp.concatenate([mult_real, mult_imag], axis=1)
    multipliers = broadcast(multipliers, "col", 0)
    pivot_block = complex_block(pivot_sum[:, :panel_width], pivot_sum[:, panel_width:])
    update = jnp.dot(multipliers, pivot_block, preferred_element_type=jnp.float32)
    updated = coupling - update
    return jnp.stack([updated[:, :panel_width], updated[:, panel_width:]]).reshape(
        2, 1, 1, owned_rows, panel_width
    )


def solution(mesh):
    return jax.shard_map(
        body,
        mesh=mesh,
        in_specs=(
            P(None, "row", "shell"),
            P(None, "shell", "col"),
            P("shell"),
            P("shell"),
            P(),
            P(),
            P(),
        ),
        out_specs=P(None, "row", "shell", None, "col"),
        check_vma=False,
    )
```

profile of v0, /device:TPU:4, one launch (start us, length us, event | category | flops | bytes accessed | tf_op | source)
XLA Modules:
  0.0 509.2 jit_solution(4400206457405959289)
XLA Ops:
  6.5 0.0 copy-start.1
  6.5 0.0 reduce-scatter.2.cloned.1.call-start
  6.5 0.8 slice_bitcast_fusion.4
  7.4 0.8 select_reduce_fusion.1
  8.1 0.7 fusion.44
  8.8 0.0 copy-start.3
  8.8 1.9 fusion.42
  10.8 0.0 copy-done.1
  10.8 0.4 fusion.18
  11.2 0.0 copy-done.3
  11.2 0.2 slice_bitcast_fusion.1
  11.4 5.3 %fusion = f32[1024,1024]{1,0:T(8,128)} fusion(bf16[1024,768]{1,0:T(8,128)(2,1)S(1)} %get-tuple-element.12, bf16[1024,768]{1,0:T(8,128)(2,1)S(1)} %get-tuple-element.11, bf16[768,512]{1,0:T(8,128)(2,1)S(1)} %fusion.18, bf16[768,512]{1,0:T(8,128)(2,1)S(1)} %get-tuple-element.9, bf16[768,512]{1,0:T(8,128)(2,1)S(1)} %get-tuple-element.10), kind=kOutput, calls=%fused_computation.1 | convolution fusion | flops 3240099840 | bytes 9699328 | tf_op jit(solution)/shard_map/dot_general | solution.py:70
  16.7 0.0 copy-start.5
  16.7 0.0 reduce-scatter.2.cloned.1.call-update
  16.8 0.0 all-reduce.5.cloned.1.call-start
  16.8 0.6 copy-done.5
  17.4 62.8 %reduce-scatter.2.cloned.1.call-done = f32[128,1024]{1,0:T(8,128)} async-done(((f32[1024,1024]{1,0:T(8,128)}), f32[128,1024]{1,0:T(8,128)}) %reduce-scatter.2.cloned.1.call-update) | async-done | bytes 524304 | tf_op jit(solution)/shard_map/reduce_scatter | solution.py:37
  80.3 3.8 gather_fusion
  84.0 0.0 copy-start
  84.0 0.0 copy-start.2
  84.1 1.4 select_convert_fusion
  85.4 0.0 all-reduce.5.cloned.1.call-update
  85.4 0.0 all-reduce.3.cloned.1.call-start
  85.5 0.0 copy-done
  85.5 0.2 copy-done.2
  85.7 0.4 fusion.30
  86.1 0.4 fusion.26
  86.4 0.4 fusion.24
  86.8 0.4 fusion.25
  87.2 0.8 maximum_select_fusion
  88.0 0.0 all-reduce.3.cloned.1.call-update
  88.0 267.2 %all-reduce.5.cloned.1.call-done = bf16[512,1024]{1,0:T(8,128)(2,1)} async-done(((bf16[512,1024]{1,0:T(8,128)(2,1)}), bf16[512,1024]{1,0:T(8,128)(2,1)}) %all-reduce.5.cloned.1.call-update) | async-done | bytes 1048592 | tf_op jit(solution)/shard_map/psum | solution.py:55
  355.2 0.0 copy-start.4
  355.2 1.4 slice_negate_fusion
  356.6 143.8 %all-reduce.3.cloned.1.call-done = bf16[128,1024]{1,0:T(8,128)(2,1)} async-done(((bf16[128,1024]{1,0:T(8,128)(2,1)}), bf16[128,1024]{1,0:T(8,128)(2,1)}) %all-reduce.3.cloned.1.call-update) | async-done | bytes 262160 | tf_op jit(solution)/shard_map/psum | solution.py:9
  500.4 0.0 copy-done.4
  500.4 1.4 fusion.21
  501.8 0.8 maximum_bitcast_fusion
  (3 shorter events, 0.1 us)
Async XLA Ops:
  6.5 4.2 copy-start.1
  6.5 73.7 %reduce-scatter.2.cloned.1.call-start = ((), (), s32[]{:S(2)}) async-start(), calls=%async_computation.1 | async-start | bytes 4718592 | tf_op jit(solution)/shard_map/reduce_scatter | solution.py:37
  8.8 2.4 copy-start.3
  16.7 0.7 copy-start.5
  16.8 338.4 %all-reduce.5.cloned.1.call-start = ((), (), s32[]{:S(2)}) async-start(), calls=%async_computation.3 | async-start | bytes 2097152 | tf_op jit(solution)/shard_map/psum | solution.py:55
  84.0 1.5 copy-start
  84.0 1.6 copy-start.2
  85.4 414.9 %all-reduce.3.cloned.1.call-start = ((), (), s32[]{:S(2)}) async-start(), calls=%async_computation.2 | async-start | bytes 524288 | tf_op jit(solution)/shard_map/psum | solution.py:9
  355.2 145.2 %copy-start.4 = (bf16[512,1024]{1,0:T(8,128)(2,1)S(1)}, bf16[512,1024]{1,0:T(8,128)(2,1)}, u32[]{:S(2)}) copy-start(bf16[512,1024]{1,0:T(8,128)(2,1)} %all-reduce.5.cloned.1.call-done) | copy-start | bytes 3145732
Sparse Core Ops, SparseCore 0:
  16.9 63.3 reduce-scatter.1
  85.6 269.6 all-reduce.4
  358.4 141.9 all-reduce.2
where the time goes:
time: 509 us
  waiting for transfers between devices  474 us (93%)
  between operations  13.2 us (3%)
  matrix products  8.23 us (2%)
  other arithmetic  8.1 us (2%)
  local copies, waits for them, and re-layouts  5.65 us (1%)
    psum x1, waiting for transfers between devices, select_pivots(): lax.psum(picked, ('shell', 'row')).astype(jnp.float32).astype(jnp.bfloat16)  267 us
    psum x1, waiting for transfers between devices, broadcast(): return lax.psum(block, axis)  144 us
    reduce_scatter x1, waiting for transfers between devices, reduce_tiles(): lax.psum_scatter(term_rows(jnp.int32(0), owned_rows * lax.axis_size('shel...  62.8 us
  transfers between devices with their start and end apart: 3, of which 3 were waited for; matrix products, arithmetic and copies ran while one was open for 1% of the time, Pallas kernels for 0%

commit v1 on v0

--- a/solution.py
+++ b/solution.py
@@ -52,7 +52,7 @@
 
 def select_pivots(coupling, pivot_rows, row_base):
     picked = pick_rows(coupling, pivot_rows, row_base).astype(jnp.bfloat16)
-    return lax.psum(picked, ("shell", "row")).astype(jnp.float32).astype(jnp.bfloat16)
+    return lax.psum(lax.psum(picked, "shell"), "row").astype(jnp.float32).astype(jnp.bfloat16)
 
 
 def body(left_basis, right_basis, point_weight, shell_index, green_table, pivot_rows, diag_inverse):

time: 509 us -> 374 us (0.73)
  waiting for transfers between devices: 474 us -> 338 us
    psum x1 -> x2, waiting for transfers between devices: 267 us -> 133 us  [the longest x1 80.4 us: select_pivots(): lax.psum(picked, 'shell')]
  transfers between devices with their start and end apart: 3 -> 4, of which waited for: 3 -> 4; matrix products, arithmetic and copies ran while one was open for 1% -> 1% of each run, Pallas kernels for 0% -> 0%
where the time goes in v1:
time: 374 us
  waiting for transfers between devices  338 us (90%)
  between operations  13.3 us (4%)
  matrix products  8.23 us (2%)
  other arithmetic  8.1 us (2%)
  local copies, waits for them, and re-layouts  5.46 us (1%)
    psum x1, waiting for transfers between devices, broadcast(): return lax.psum(block, axis)  142 us
    psum x1, waiting for transfers between devices, select_pivots(): lax.psum(picked, 'shell')  80.4 us
    reduce_scatter x1, waiting for transfers between devices, reduce_tiles(): lax.psum_scatter(term_rows(jnp.int32(0), owned_rows * lax.axis_size('shel...  62.8 us
    psum x1, waiting for transfers between devices, select_pivots(): lax.psum(lax.psum(picked, 'shell'), 'row').astype(jnp.float32)  52.7 us
  transfers between devices with their start and end apart: 4, of which 4 were waited for; matrix products, arithmetic and copies ran while one was open for 1% of the time, Pallas kernels for 0%

profile of v1, /device:TPU:4, one launch (start us, length us, event | category | flops | bytes accessed | tf_op | source)
XLA Modules:
  0.0 373.6 jit_solution(9171483931521371890)
XLA Ops:
  6.5 0.0 copy-start.1
  6.5 0.0 reduce-scatter.2.cloned.1.call-start
  6.5 0.8 slice_bitcast_fusion.4
  7.4 0.8 select_reduce_fusion.1
  8.1 0.7 fusion.44
  8.8 0.0 copy-start.3
  8.8 1.9 fusion.42
  10.8 0.0 copy-done.1
  10.8 0.4 fusion.18
  11.2 0.0 copy-done.3
  11.2 0.2 slice_bitcast_fusion.1
  11.4 5.3 %fusion = f32[1024,1024]{1,0:T(8,128)} fusion(bf16[1024,768]{1,0:T(8,128)(2,1)S(1)} %get-tuple-element.12, bf16[1024,768]{1,0:T(8,128)(2,1)S(1)} %get-tuple-element.11, bf16[768,512]{1,0:T(8,128)(2,1)S(1)} %fusion.18, bf16[768,512]{1,0:T(8,128)(2,1)S(1)} %get-tuple-element.9, bf16[768,512]{1,0:T(8,128)(2,1)S(1)} %get-tuple-element.10), kind=kOutput, calls=%fused_computation.1 | convolution fusion | flops 3240099840 | bytes 9699328 | tf_op jit(solution)/shard_map/dot_general | solution.py:70
  16.7 0.0 copy-start.5
  16.7 0.0 reduce-scatter.2.cloned.1.call-update
  16.8 0.0 all-reduce.6.cloned.1.call-start
  16.8 0.6 copy-done.5
  17.4 62.8 %reduce-scatter.2.cloned.1.call-done = f32[128,1024]{1,0:T(8,128)} async-done(((f32[1024,1024]{1,0:T(8,128)}), f32[128,1024]{1,0:T(8,128)}) %reduce-scatter.2.cloned.1.call-update) | async-done | bytes 524304 | tf_op jit(solution)/shard_map/reduce_scatter | solution.py:37
  80.3 3.8 %gather_fusion = bf16[512,1024]{1,0:T(8,128)(2,1)S(1)} fusion(f32[128,1024]{1,0:T(8,128)} %reduce-scatter.2.cloned.1.call-done, s32[1024]{0:T(1024)S(1)} %pad_clamp_fusion), kind=kCustom, calls=%fused_computation | custom fusion | bytes 2099200 | tf_op jit(solution)/shard_map/jit(_take)/gather | solution.py:49
  84.0 0.0 copy-start
  84.0 0.0 copy-start.2
  84.1 1.4 select_convert_fusion
  85.4 0.0 all-reduce.6.cloned.1.call-update
  85.4 0.0 all-reduce.8.cloned.1.call-start
  85.5 80.4 %all-reduce.6.cloned.1.call-done = bf16[512,1024]{1,0:T(8,128)(2,1)} async-done(((bf16[512,1024]{1,0:T(8,128)(2,1)}), bf16[512,1024]{1,0:T(8,128)(2,1)}) %all-reduce.6.cloned.1.call-update) | async-done | bytes 1048592 | tf_op jit(solution)/shard_map/psum | solution.py:55
  165.9 0.0 all-reduce.8.cloned.1.call-update
  165.9 0.0 all-reduce.4.cloned.1.call-start
  165.9 0.0 copy-done
  166.0 0.0 copy-done.2
  166.0 0.4 fusion.30
  166.3 0.4 fusion.26
  166.7 0.4 fusion.24
  167.1 0.4 fusion.25
  167.5 0.8 maximum_select_fusion
  168.3 0.0 all-reduce.4.cloned.1.call-update
  168.3 52.7 %all-reduce.8.cloned.1.call-done = bf16[512,1024]{1,0:T(8,128)(2,1)} async-done(((bf16[512,1024]{1,0:T(8,128)(2,1)}), bf16[512,1024]{1,0:T(8,128)(2,1)}) %all-reduce.8.cloned.1.call-update) | async-done | bytes 1048592 | tf_op jit(solution)/shard_map/psum | solution.py:55
  221.0 0.0 copy-start.4
  221.0 1.4 slice_negate_fusion
  222.3 142.4 %all-reduce.4.cloned.1.call-done = bf16[128,1024]{1,0:T(8,128)(2,1)} async-done(((bf16[128,1024]{1,0:T(8,128)(2,1)}), bf16[128,1024]{1,0:T(8,128)(2,1)}) %all-reduce.4.cloned.1.call-update) | async-done | bytes 262160 | tf_op jit(solution)/shard_map/psum | solution.py:9
  364.8 0.0 copy-done.4
  364.8 1.4 fusion.21
  366.2 0.8 maximum_bitcast_fusion
  (3 shorter events, 0.1 us)
Async XLA Ops:
  6.5 4.2 %copy-start.1 = (bf16[2,768,512]{2,1,0:T(8,128)(2,1)S(1)}, bf16[2,768,512]{2,1,0:T(8,128)(2,1)}, u32[]{:S(2)}) copy-start(bf16[2,768,512]{2,1,0:T(8,128)(2,1)} %param.8) | copy-start | bytes 4718596
  6.5 73.7 %reduce-scatter.2.cloned.1.call-start = ((), (), s32[]{:S(2)}) async-start(), calls=%async_computation.1 | async-start | bytes 4718592 | tf_op jit(solution)/shard_map/reduce_scatter | solution.py:37
  8.8 2.4 copy-start.3
  16.7 0.7 copy-start.5
  16.8 149.1 %all-reduce.6.cloned.1.call-start = ((), (), s32[]{:S(2)}) async-start(), calls=%async_computation.3 | async-start | bytes 2097152 | tf_op jit(solution)/shard_map/psum | solution.py:55
  84.0 81.9 %copy-start = (f32[128,1024]{1,0:T(8,128)S(1)}, f32[128,1024]{1,0:T(8,128)}, u32[]{:S(2)}) copy-start(f32[128,1024]{1,0:T(8,128)} %reduce-scatter.2.cloned.1.call-done) | copy-start | bytes 1572868
  84.0 81.9 %copy-start.2 = (bf16[2,512,512]{2,1,0:T(8,128)(2,1)S(1)}, bf16[2,512,512]{2,1,0:T(8,128)(2,1)}, u32[]{:S(2)}) copy-start(bf16[2,512,512]{2,1,0:T(8,128)(2,1)} %param.13) | copy-start | bytes 3145732
  85.4 135.5 %all-reduce.8.cloned.1.call-start = ((), (), s32[]{:S(2)}) async-start(), calls=%async_computation.4 | async-start | bytes 2097152 | tf_op jit(solution)/shard_map/psum | solution.py:55
  165.9 198.9 %all-reduce.4.cloned.1.call-start = ((), (), s32[]{:S(2)}) async-start(), calls=%async_computation.2 | async-start | bytes 524288 | tf_op jit(solution)/shard_map/psum | solution.py:9
  221.0 143.8 %copy-start.4 = (bf16[512,1024]{1,0:T(8,128)(2,1)S(1)}, bf16[512,1024]{1,0:T(8,128)(2,1)}, u32[]{:S(2)}) copy-start(bf16[512,1024]{1,0:T(8,128)(2,1)} %all-reduce.8.cloned.1.call-done) | copy-start | bytes 3145732
Sparse Core Ops, SparseCore 0:
  16.9 63.3 reduce-scatter.1
  85.6 80.2 all-reduce.5
  168.8 52.0 all-reduce.7
  224.0 140.7 all-reduce.3

commit v2 on v0

--- a/solution.py
+++ b/solution.py
@@ -52,7 +52,11 @@
 
 def select_pivots(coupling, pivot_rows, row_base):
     picked = pick_rows(coupling, pivot_rows, row_base).astype(jnp.bfloat16)
-    return lax.psum(picked, ("shell", "row")).astype(jnp.float32).astype(jnp.bfloat16)
+    return (
+        jnp.sum(lax.all_gather(picked, ("shell", "row")), axis=0)
+        .astype(jnp.float32)
+        .astype(jnp.bfloat16)
+    )
 
 
 def body(left_basis, right_basis, point_weight, shell_index, green_table, pivot_rows, diag_inverse):

time: 509 us -> 465 us (0.914)
  waiting for transfers between devices: 474 us -> 419 us
  other arithmetic: 8.1 us -> 18.3 us
    psum x1 -> x0, waiting for transfers between devices: 267 us -> none  [select_pivots(): lax.psum(picked, ('shell', 'row')).astype(jnp.float32).astype(jnp.bfloat16)]
    all_gather x0 -> x1, waiting for transfers between devices: none -> 227 us  [select_pivots(): lax.all_gather(picked, ('shell', 'row'))]
    psum x1, waiting for transfers between devices: 144 us -> 129 us  [broadcast(): return lax.psum(block, axis)]
    reduce_sum x0 -> x1, other arithmetic: none -> 11.5 us  [select_pivots(): jnp.sum(lax.all_gather(picked, ('shell', 'row')), axis=0)]
  transfers between devices with their start and end apart: 3 -> 3, of which waited for: 3 -> 3; matrix products, arithmetic and copies ran while one was open for 1% -> 3% of each run, Pallas kernels for 0% -> 0%
where the time goes in v2:
time: 465 us; the launch traced here: 464 us
  waiting for transfers between devices  419 us (90%)
  other arithmetic  18.3 us (4%)
  between operations  13.3 us (3%)
  matrix products  8.23 us (2%)
  local copies, waits for them, and re-layouts  5.69 us (1%)
    all_gather x1, waiting for transfers between devices, select_pivots(): lax.all_gather(picked, ('shell', 'row'))  227 us
    psum x1, waiting for transfers between devices, broadcast(): return lax.psum(block, axis)  129 us
    reduce_scatter x1, waiting for transfers between devices, reduce_tiles(): lax.psum_scatter(term_rows(jnp.int32(0), owned_rows * lax.axis_size('shel...  62.8 us
    reduce_sum x1, other arithmetic, select_pivots(): jnp.sum(lax.all_gather(picked, ('shell', 'row')), axis=0)  11.5 us
  transfers between devices with their start and end apart: 3, of which 3 were waited for; matrix products, arithmetic and copies ran while one was open for 3% of the time, Pallas kernels for 0%

profile of v2, /device:TPU:4, one launch (start us, length us, event | category | flops | bytes accessed | tf_op | source)
XLA Modules:
  0.0 464.5 jit_solution(2071540311526868241)
XLA Ops:
  6.5 0.0 copy-start.1
  6.5 0.0 reduce-scatter.2.cloned.1.call-start
  6.5 0.8 slice_bitcast_fusion.4
  7.4 0.8 select_reduce_fusion.1
  8.1 0.7 fusion.46
  8.8 0.0 copy-start.3
  8.8 1.9 fusion.44
  10.8 0.0 copy-done.1
  10.8 0.4 fusion.20
  11.2 0.0 copy-done.3
  11.2 0.2 slice_bitcast_fusion.1
  11.4 5.3 %fusion = f32[1024,1024]{1,0:T(8,128)} fusion(bf16[1024,768]{1,0:T(8,128)(2,1)S(1)} %get-tuple-element.12, bf16[1024,768]{1,0:T(8,128)(2,1)S(1)} %get-tuple-element.11, bf16[768,512]{1,0:T(8,128)(2,1)S(1)} %fusion.20, bf16[768,512]{1,0:T(8,128)(2,1)S(1)} %get-tuple-element.9, bf16[768,512]{1,0:T(8,128)(2,1)S(1)} %get-tuple-element.10), kind=kOutput, calls=%fused_computation.1 | convolution fusion | flops 3240099840 | bytes 9699328 | tf_op jit(solution)/shard_map/dot_general | solution.py:74
  16.7 0.0 copy-start.4
  16.7 0.0 reduce-scatter.2.cloned.1.call-update
  16.8 0.0 all-gather.2.cloned.1.call-start
  16.8 0.6 copy-done.4
  17.4 62.8 %reduce-scatter.2.cloned.1.call-done = f32[128,1024]{1,0:T(8,128)} async-done(((f32[1024,1024]{1,0:T(8,128)}), f32[128,1024]{1,0:T(8,128)}) %reduce-scatter.2.cloned.1.call-update) | async-done | bytes 524304 | tf_op jit(solution)/shard_map/reduce_scatter | solution.py:37
  80.3 3.8 gather_fusion
  84.0 0.0 copy-start
  84.0 0.0 copy-start.2
  84.1 1.3 fusion.18
  85.4 0.0 all-gather.2.cloned.1.call-update
  85.4 0.0 all-reduce.2.cloned.1.call-start
  85.4 0.0 copy-done
  85.5 0.2 copy-done.2
  85.7 0.4 fusion.32
  86.1 0.4 fusion.28
  86.5 0.4 fusion.26
  86.8 0.4 fusion.27
  87.2 0.8 maximum_select_fusion
  88.0 0.0 all-reduce.2.cloned.1.call-update
  88.0 227.3 %all-gather.2.cloned.1.call-done = bf16[32,512,1024]{2,1,0:T(8,128)(2,1)} async-done(((bf16[1,512,1024]{2,1,0:T(8,128)(2,1)}), bf16[32,512,1024]{2,1,0:T(8,128)(2,1)}) %all-gather.2.cloned.1.call-update) | async-done | bytes 33554448 | tf_op jit(solution)/shard_map/all_gather | solution.py:56
  315.3 11.5 %reduce_sum.32 = bf16[512,1024]{1,0:T(8,128)(2,1)S(1)} reduce(bf16[32,512,1024]{2,1,0:T(8,128)(2,1)} %all-gather.2.cloned.1.call-done, bf16[]{:T(256)} %constant.15.clone.1), dimensions={0}, to_apply=%region_4.5 | reduce | flops 16252928 | bytes 34603008 | tf_op jit(solution)/shard_map/reduce_sum | solution.py:56
  326.8 0.1 slice_negate_fusion
  326.9 128.8 %all-reduce.2.cloned.1.call-done = bf16[128,1024]{1,0:T(8,128)(2,1)} async-done(((bf16[128,1024]{1,0:T(8,128)(2,1)}), bf16[128,1024]{1,0:T(8,128)(2,1)}) %all-reduce.2.cloned.1.call-update) | async-done | bytes 262160 | tf_op jit(solution)/shard_map/psum | solution.py:9
  455.7 1.4 fusion.23
  457.1 0.8 maximum_bitcast_fusion
  (3 shorter events, 0.1 us)
Async XLA Ops:
  6.5 4.2 copy-start.1
  6.5 73.7 %reduce-scatter.2.cloned.1.call-start = ((), (), s32[]{:S(2)}) async-start(), calls=%async_computation.1 | async-start | bytes 4718592 | tf_op jit(solution)/shard_map/reduce_scatter | solution.py:37
  8.8 2.4 copy-start.3
  16.7 0.7 copy-start.4
  16.8 298.6 %all-gather.2.cloned.1.call-start = ((), (), s32[]{:S(2)}) async-start(), calls=%async_computation.3 | async-start | bytes 34603008 | tf_op jit(solution)/shard_map/all_gather | solution.py:56
  84.0 1.4 copy-start
  84.0 1.6 copy-start.2
  85.4 370.3 %all-reduce.2.cloned.1.call-start = ((), (), s32[]{:S(2)}) async-start(), calls=%async_computation.2 | async-start | bytes 524288 | tf_op jit(solution)/shard_map/psum | solution.py:9
Sparse Core Ops, SparseCore 0:
  16.9 63.3 reduce-scatter.1
  85.5 229.7 all-gather.1
  318.2 137.3 all-reduce.1
